TPU v7x, 512 devices: a whole 4x4x16 slice. The times are simulated.
512 devices in a mesh: line: 32 (over x, y, core), seg: 16 (over z).
Axes of the slice: x: 4, y: 4, z: 16, core: 2. Of those that a mesh axis runs over, the one named last changes fastest.
Arguments:
- points: float32 [32, 16, 3, 32768], P('line', 'seg'), may hold values from -1 to 1
- rows: int32 [32, 16, 2, 3072], P('line', 'seg'), may hold values from -1 to 32767, as said below
- cells: int32 [32, 16, 2, 24], P('line', 'seg'), may hold values from -1 to 15, as said below
- pose: float32 [12, 32], P(None, 'line'), as said below
Outputs:
- matched: float32 [32, 16, 2, 5, 3072], P('line', 'seg')
- fitted_pose: float32 [12, 32], P(None, 'line')
- final_spread: float32 [1], replicated
Inputs may be any that keep to these rules, and one draw needn't show every extreme that they name: In each block of 128 slots the filled slots come first; every slot of an empty block is empty; rows toward the lower line lie in the lower margin (below 8192), rows toward the upper line in the upper margin (24576 or more); the lists of line 0 toward the lower side and of line 32 - 1 toward the upper side are empty. `cells`: empty blocks come after the others; in segment 0 of every line all blocks toward an existing adjacent line are filled. `pose`: every 3x3 part is within about 0.5 of the identity.
All inputs are finite; a program needn't handle non-finite values.
Results may differ from a plain program's by a relative error of at most 0.0003.
Values sent between devices are 32-bit elements; how exact they have to be, the bound alone decides.
A program may use at most 64 MiB of HBM per device.

v0:
```python
import jax
import jax.numpy as jnp
from jax import lax
from jax.sharding import PartitionSpec as P

NCELL = 16
CT = 512
BLOCK = 128
ITERS = 2
OUTLIER_MASS = 1.0
SPREAD_START = 0.05
PRIOR_TOP = 0.05
PRIOR_BOTTOM = 1.0
REGULARIZE = 1.0
blocks_per_turn = 4


def from_behind(value, axis, steps):
    count = lax.axis_size(axis)
    initial, last = (max(0, -steps), min(count, count - steps))
    return lax.ppermute(value, axis, [(source, source + steps) for source in range(initial, last)])


def match_block(source_block, cell_id, world_points, spread):
    first_column = jnp.maximum(cell_id, 0) * CT
    target = lax.dynamic_slice_in_dim(world_points, first_column, CT, 1)
    distance = (source_block[0][:, None] - target[0][None, :]) ** 2
    distance = distance + (source_block[1][:, None] - target[1][None, :]) ** 2
    distance = distance + (source_block[2][:, None] - target[2][None, :]) ** 2
    weight = jnp.exp(-distance / (2.0 * spread))
    total_weight = jnp.sum(weight, axis=1)
    posterior = weight / (total_weight + OUTLIER_MASS)[:, None]
    pulled = lax.dot_general(
        target,
        posterior,
        (((1,), (1,)), ((), ())),
        precision=lax.Precision.HIGHEST,
        preferred_element_type=jnp.float32,
    )
    share_row = total_weight / (total_weight + OUTLIER_MASS)
    energy_row = jnp.sum(posterior * distance, axis=1)
    merged_rows = jnp.concatenate([pulled, share_row[None, :], energy_row[None, :]], axis=0)
    return jnp.where(cell_id >= 0, merged_rows, jnp.zeros_like(merged_rows))


def match_all(sources, block_cells, worlds, spread):
    block_total = block_cells.shape[1]
    turns = 2 * block_total // blocks_per_turn
    grouped = (
        sources.reshape(2, 3, block_total, BLOCK)
        .transpose(0, 2, 1, 3)
        .reshape(turns, blocks_per_turn, 3, BLOCK)
    )
    grouped_cells = block_cells.reshape(turns, blocks_per_turn)
    sides = jnp.arange(turns) // (turns // 2)

    def one_turn(packed):
        turn_blocks, turn_cells, side = packed
        target_world = lax.dynamic_index_in_dim(worlds, side, 0, keepdims=False)

        def compute(unused):
            return jax.vmap(
                lambda block_points, block_cell: match_block(
                    block_points, block_cell, target_world, spread
                )
            )(turn_blocks, turn_cells)

        def skipped(unused):
            return jnp.zeros((blocks_per_turn, 5, BLOCK), jnp.float32)

        return lax.cond(jnp.any(turn_cells >= 0), compute, skipped, 0)

    output = lax.map(one_turn, (grouped, grouped_cells, sides))
    return (
        output.reshape(2, block_total, 5, BLOCK)
        .transpose(0, 2, 1, 3)
        .reshape(2, 5, block_total * BLOCK)
    )


def solve_pose(gram_matrix, cross_matrix, pose_column):
    old_pose = jnp.concatenate(
        [pose_column[:9].reshape(3, 3), pose_column[9:].reshape(3, 1)], axis=1
    )
    left_side = gram_matrix + REGULARIZE * jnp.eye(4, dtype=gram_matrix.dtype)
    right_side = cross_matrix + REGULARIZE * old_pose
    factor = jnp.linalg.cholesky(left_side)
    solved = jax.scipy.linalg.cho_solve((factor, True), right_side.T)
    new_pose = solved.T
    return jnp.concatenate([new_pose[:, :3].reshape(9), new_pose[:, 3]])


def send_lists(lists, marks, step):
    return from_behind((lists, marks), "line", step)


def send_back(piece, step):
    return from_behind(piece, "line", step)


def on_device(points, rows, cells, pose):
    own_points = points[0, 0]
    row_list = rows[0, 0]
    cell_ids = cells[0, 0]
    pose_column = pose[:, 0]
    margin = NCELL * CT
    point_total = own_points.shape[1]
    slot_total = row_list.shape[1]
    live_slots = (row_list >= 0).astype(jnp.float32)
    safe_rows = jnp.where(row_list >= 0, row_list, 0)
    raw_source = (
        jnp.take(own_points, safe_rows.reshape(-1), axis=1)
        .reshape(3, 2, slot_total)
        .transpose(1, 0, 2)
    )
    extended = jnp.concatenate([raw_source, jnp.ones((2, 1, slot_total), jnp.float32)], axis=1)
    spread = jnp.float32(SPREAD_START)
    result = None
    for iteration in range(ITERS):
        linear_part = pose_column[:9].reshape(3, 3)
        offset_part = pose_column[9:]
        world_points = (
            jnp.dot(
                linear_part,
                own_points,
                precision=lax.Precision.HIGHEST,
                preferred_element_type=jnp.float32,
            )
            + offset_part[:, None]
        )
        moved_source = (
            jnp.einsum("km,dms->dks", linear_part, raw_source, precision=lax.Precision.HIGHEST)
            + offset_part[None, :, None]
        )
        lower_margin = world_points[:, :margin]
        upper_margin = world_points[:, point_total - margin :]
        cell_marks = (cell_ids + 1).astype(jnp.float32)
        lists_down, marks_down = send_lists(moved_source[0], cell_marks[0], -1)
        lists_up, marks_up = send_lists(moved_source[1], cell_marks[1], 1)
        incoming = jnp.stack([lists_down, lists_up])
        got_cells = jnp.stack([marks_down, marks_up]).astype(jnp.int32) - 1
        own_worlds = jnp.stack([upper_margin, lower_margin])
        answers = match_all(incoming, got_cells, own_worlds, spread)
        result = jnp.stack([send_back(answers[0], 1), send_back(answers[1], -1)])
        result = result * live_slots[:, None, :]
        pulled = result[:, :3]
        share_all = result[:, 3]
        energy_all = result[:, 4]
        gram_matrix = jnp.einsum(
            "dks,dms->km",
            extended * share_all[:, None, :],
            extended,
            precision=lax.Precision.HIGHEST,
        )
        cross_matrix = jnp.einsum("dks,dms->km", pulled, extended, precision=lax.Precision.HIGHEST)
        energy_part = jnp.sum(energy_all)
        share_part = jnp.sum(share_all)
        gram_sum, cross_sum = lax.psum((gram_matrix, cross_matrix), "seg")
        energy_sum, share_sum = lax.psum((energy_part, share_part), ("line", "seg"))
        pose_column = solve_pose(gram_sum, cross_sum, pose_column)
        spread = (energy_sum + PRIOR_TOP) / (3.0 * share_sum + PRIOR_BOTTOM)
    return (result[None, None], pose_column[:, None], spread.reshape(1))


def solution(mesh):
    return jax.shard_map(
        on_device,
        mesh=mesh,
        in_specs=(
            P("line", "seg", None, None),
            P("line", "seg", None, None),
            P("line", "seg", None, None),
            P(None, "line"),
        ),
        out_specs=(P("line", "seg", None, None, None), P(None, "line"), P()),
        check_vma=False,
    )
```

profile of v0, /device:TPU:2, one launch (start us, length us, event | category | flops | bytes accessed | tf_op | source)
XLA Modules:
  0.0 667.9 jit_solution(6395573650611481252)
XLA Ops:
  13.1 21.8 %gather_fusion = f32[6144,3]{1,0:T(8,128)S(1)} fusion(f32[3,32768]{0,1:T(8,128)} %bitcast.285, s32[6144]{0:T(1024)S(1)} %broadcast_clamp_fusion), kind=kCustom, calls=%fused_computation | custom fusion | bytes 172032 | tf_op jit(solution)/shard_map/jit(_take)/gather | solution.py:112
  48.7 16.7 %convolution_add_fusion.1 = f32[3,32768]{1,0:T(4,128)S(1)} fusion(f32[3,3]{1,0:T(4,128)S(1)} %reshape.263, f32[3]{0:T(128)S(1)} %get-tuple-element.442, f32[1,1,3,32768]{2,3,1,0:T(8,128)} %copy.18), kind=kOutput, calls=%fused_computation.61 | convolution fusion | flops 3637248 | bytes 786480 | tf_op jit(solution)/shard_map/dot_general | solution.py:123
  65.8 139.7 %while.28 = (s32[]{:T(128)}, f32[12,4,5,128]{3,2,1,0:T(8,128)S(1)}, s32[12,4]{1,0:T(8,128)S(1)}, f32[2,3,8192]{2,1,0:T(4,128)S(1)}, f32[12,4,3,128]{3,1,2,0:T(4,128)S(1)}, /*index=5*/s32[]{:T(128)}, s32[]{:T(128)}, s32[]{:T(128)}) while((s32[]{:T(128)}, f32[12,4,5,128]{3,2,1,0:T(8,128)S(1)}, s32[12,4]{1,0:T(8,128)S(1)}, ...), condition=%wide.region_6.7_spmd.clone, body=%wide.region_0.6_spmd.clone.sunk | while | flops 18620548 | bytes 529362 | solution.py:73
  67.1 10.3 %conditional.6 = (f32[1,4,5,128]{3,2,1,0:T(8,128)S(1)}) conditional(s32[]{:T(128)} %convert_element_type.49, () %tuple.138, (s32[4]{0:T(128)S(1)}, s32[12]{0:T(128)S(1)}, s32[]{:T(128)}, f32[2,3,8192]{2,1,0:T(4,128)S(1)}, f32[12,4,3,128]{3,1,2,0:T(4,128)S(1)}, /*index=5*/s32[12]{0:T(128)S(1)}, s32[12]{0:T(128)S(1)}, s32[12]{0:T(128)S(1)}, ...), branch_computations={%region_2.2_spmd, %region_3.5_spmd.clone} | conditional | flops 18620528 | bytes 496227 | solution.py:71
  78.7 10.3 %conditional.6 = (f32[1,4,5,128]{3,2,1,0:T(8,128)S(1)}) conditional(s32[]{:T(128)} %convert_element_type.49, () %tuple.138, (s32[4]{0:T(128)S(1)}, s32[12]{0:T(128)S(1)}, s32[]{:T(128)}, f32[2,3,8192]{2,1,0:T(4,128)S(1)}, f32[12,4,3,128]{3,1,2,0:T(4,128)S(1)}, /*index=5*/s32[12]{0:T(128)S(1)}, s32[12]{0:T(128)S(1)}, s32[12]{0:T(128)S(1)}, ...), branch_computations={%region_2.2_spmd, %region_3.5_spmd.clone} | conditional | flops 18620528 | bytes 496227 | solution.py:71
  90.4 10.3 %conditional.6 = (f32[1,4,5,128]{3,2,1,0:T(8,128)S(1)}) conditional(s32[]{:T(128)} %convert_element_type.49, () %tuple.138, (s32[4]{0:T(128)S(1)}, s32[12]{0:T(128)S(1)}, s32[]{:T(128)}, f32[2,3,8192]{2,1,0:T(4,128)S(1)}, f32[12,4,3,128]{3,1,2,0:T(4,128)S(1)}, /*index=5*/s32[12]{0:T(128)S(1)}, s32[12]{0:T(128)S(1)}, s32[12]{0:T(128)S(1)}, ...), branch_computations={%region_2.2_spmd, %region_3.5_spmd.clone} | conditional | flops 18620528 | bytes 496227 | solution.py:71
  102.0 10.3 %conditional.6 = (f32[1,4,5,128]{3,2,1,0:T(8,128)S(1)}) conditional(s32[]{:T(128)} %convert_element_type.49, () %tuple.138, (s32[4]{0:T(128)S(1)}, s32[12]{0:T(128)S(1)}, s32[]{:T(128)}, f32[2,3,8192]{2,1,0:T(4,128)S(1)}, f32[12,4,3,128]{3,1,2,0:T(4,128)S(1)}, /*index=5*/s32[12]{0:T(128)S(1)}, s32[12]{0:T(128)S(1)}, s32[12]{0:T(128)S(1)}, ...), branch_computations={%region_2.2_spmd, %region_3.5_spmd.clone} | conditional | flops 18620528 | bytes 496227 | solution.py:71
  113.7 10.3 %conditional.6 = (f32[1,4,5,128]{3,2,1,0:T(8,128)S(1)}) conditional(s32[]{:T(128)} %convert_element_type.49, () %tuple.138, (s32[4]{0:T(128)S(1)}, s32[12]{0:T(128)S(1)}, s32[]{:T(128)}, f32[2,3,8192]{2,1,0:T(4,128)S(1)}, f32[12,4,3,128]{3,1,2,0:T(4,128)S(1)}, /*index=5*/s32[12]{0:T(128)S(1)}, s32[12]{0:T(128)S(1)}, s32[12]{0:T(128)S(1)}, ...), branch_computations={%region_2.2_spmd, %region_3.5_spmd.clone} | conditional | flops 18620528 | bytes 496227 | solution.py:71
  125.3 10.3 %conditional.6 = (f32[1,4,5,128]{3,2,1,0:T(8,128)S(1)}) conditional(s32[]{:T(128)} %convert_element_type.49, () %tuple.138, (s32[4]{0:T(128)S(1)}, s32[12]{0:T(128)S(1)}, s32[]{:T(128)}, f32[2,3,8192]{2,1,0:T(4,128)S(1)}, f32[12,4,3,128]{3,1,2,0:T(4,128)S(1)}, /*index=5*/s32[12]{0:T(128)S(1)}, s32[12]{0:T(128)S(1)}, s32[12]{0:T(128)S(1)}, ...), branch_computations={%region_2.2_spmd, %region_3.5_spmd.clone} | conditional | flops 18620528 | bytes 496227 | solution.py:71
  136.9 10.3 %conditional.6 = (f32[1,4,5,128]{3,2,1,0:T(8,128)S(1)}) conditional(s32[]{:T(128)} %convert_element_type.49, () %tuple.138, (s32[4]{0:T(128)S(1)}, s32[12]{0:T(128)S(1)}, s32[]{:T(128)}, f32[2,3,8192]{2,1,0:T(4,128)S(1)}, f32[12,4,3,128]{3,1,2,0:T(4,128)S(1)}, /*index=5*/s32[12]{0:T(128)S(1)}, s32[12]{0:T(128)S(1)}, s32[12]{0:T(128)S(1)}, ...), branch_computations={%region_2.2_spmd, %region_3.5_spmd.clone} | conditional | flops 18620528 | bytes 496227 | solution.py:71
  148.6 10.3 %conditional.6 = (f32[1,4,5,128]{3,2,1,0:T(8,128)S(1)}) conditional(s32[]{:T(128)} %convert_element_type.49, () %tuple.138, (s32[4]{0:T(128)S(1)}, s32[12]{0:T(128)S(1)}, s32[]{:T(128)}, f32[2,3,8192]{2,1,0:T(4,128)S(1)}, f32[12,4,3,128]{3,1,2,0:T(4,128)S(1)}, /*index=5*/s32[12]{0:T(128)S(1)}, s32[12]{0:T(128)S(1)}, s32[12]{0:T(128)S(1)}, ...), branch_computations={%region_2.2_spmd, %region_3.5_spmd.clone} | conditional | flops 18620528 | bytes 496227 | solution.py:71
  160.2 10.3 %conditional.6 = (f32[1,4,5,128]{3,2,1,0:T(8,128)S(1)}) conditional(s32[]{:T(128)} %convert_element_type.49, () %tuple.138, (s32[4]{0:T(128)S(1)}, s32[12]{0:T(128)S(1)}, s32[]{:T(128)}, f32[2,3,8192]{2,1,0:T(4,128)S(1)}, f32[12,4,3,128]{3,1,2,0:T(4,128)S(1)}, /*index=5*/s32[12]{0:T(128)S(1)}, s32[12]{0:T(128)S(1)}, s32[12]{0:T(128)S(1)}, ...), branch_computations={%region_2.2_spmd, %region_3.5_spmd.clone} | conditional | flops 18620528 | bytes 496227 | solution.py:71
  171.9 10.3 %conditional.6 = (f32[1,4,5,128]{3,2,1,0:T(8,128)S(1)}) conditional(s32[]{:T(128)} %convert_element_type.49, () %tuple.138, (s32[4]{0:T(128)S(1)}, s32[12]{0:T(128)S(1)}, s32[]{:T(128)}, f32[2,3,8192]{2,1,0:T(4,128)S(1)}, f32[12,4,3,128]{3,1,2,0:T(4,128)S(1)}, /*index=5*/s32[12]{0:T(128)S(1)}, s32[12]{0:T(128)S(1)}, s32[12]{0:T(128)S(1)}, ...), branch_computations={%region_2.2_spmd, %region_3.5_spmd.clone} | conditional | flops 18620528 | bytes 496227 | solution.py:71
  195.2 10.3 %conditional.6 = (f32[1,4,5,128]{3,2,1,0:T(8,128)S(1)}) conditional(s32[]{:T(128)} %convert_element_type.49, () %tuple.138, (s32[4]{0:T(128)S(1)}, s32[12]{0:T(128)S(1)}, s32[]{:T(128)}, f32[2,3,8192]{2,1,0:T(4,128)S(1)}, f32[12,4,3,128]{3,1,2,0:T(4,128)S(1)}, /*index=5*/s32[12]{0:T(128)S(1)}, s32[12]{0:T(128)S(1)}, s32[12]{0:T(128)S(1)}, ...), branch_computations={%region_2.2_spmd, %region_3.5_spmd.clone} | conditional | flops 18620528 | bytes 496227 | solution.py:71
  217.4 34.0 %all-reduce.6 = (f32[3,4]{1,0:T(4,128)S(1)}, f32[4,4]{0,1:T(4,128)S(1)}) all-reduce(f32[3,4]{1,0:T(4,128)S(1)} %convolution_bitcast_fusion.6, f32[4,4]{0,1:T(4,128)S(1)} %convolution_bitcast_fusion.7), channel_id=1, replica_groups=mesh['line'=32,'seg'=16] {'seg'}, use_global_device_ids=true, to_apply=%region_10.12 | all-reduce | flops 28 | bytes 224 | tf_op jit(solution)/shard_map/psum | solution.py:158
  254.3 16.7 %convolution_add_fusion = f32[3,32768]{1,0:T(4,128)S(1)} fusion(f32[3]{0:T(128)S(1)} %slice_reduce_fusion.3, f32[3,4]{1,0:T(4,128)S(1)} %convolution_bitcast_fusion.5, f32[1,1,3,32768]{2,3,1,0:T(8,128)} %copy.18), kind=kOutput, calls=%fused_computation.60 | convolution fusion | flops 3637248 | bytes 786492 | tf_op jit(solution)/shard_map/dot_general | solution.py:123
  278.9 98.2 %all-reduce.4 = (f32[]{:T(128)}, f32[]{:T(128)}) all-reduce(f32[]{:T(128)} %get-tuple-element.356, f32[]{:T(128)} %get-tuple-element.355), channel_id=1, replica_groups=mesh['line'=32,'seg'=16] {'line','seg'}, use_global_device_ids=true, to_apply=%region_12.15 | all-reduce | flops 2 | bytes 16 | tf_op jit(solution)/shard_map/psum | solution.py:159
  378.5 140.6 %while.29 = (s32[]{:T(128)}, f32[12,4,5,128]{3,2,1,0:T(8,128)S(1)}, s32[12,4]{1,0:T(8,128)S(1)}, f32[2,3,8192]{2,1,0:T(4,128)S(1)}, f32[12,4,3,128]{3,1,2,0:T(4,...) while((s32[]{:T(128)}, f32[12,4,5,128]{3,2,1,0:T(8,128)S(1)}, ...), condition=%wide.region_21.24_spmd.clone, body=%wide.region_15.23_spmd.clone.sunk | while | flops 18620552 | bytes 529402 | solution.py:73
  379.9 10.4 %conditional.7 = (f32[1,4,5,128]{3,2,1,0:T(8,128)S(1)}) conditional(s32[]{:T(128)} %convert_element_type.50, () %tuple.142, (s32[4]{0:T(128)S(1)}, s32[12]{0:T(128)S(1)}, s32[]{:T(128)}, f32[2,3,8192]{2,1,0:T(4,128)S(1)}, f32[12,4,3,128]{3,1,2,0:T(4,128)S(1)}, /*index=5*/f32[]{:T(128)}, s32[12]{0:T(128)S(1)}, s32[12]{0:T(128)S(1)}, ...), branch_computations={%region_17.19_spmd, %region_18.22_spmd.clone} | conditional | flops 18620530 | bytes 496251 | solution.py:71
  391.6 10.4 %conditional.7 = (f32[1,4,5,128]{3,2,1,0:T(8,128)S(1)}) conditional(s32[]{:T(128)} %convert_element_type.50, () %tuple.142, (s32[4]{0:T(128)S(1)}, s32[12]{0:T(128)S(1)}, s32[]{:T(128)}, f32[2,3,8192]{2,1,0:T(4,128)S(1)}, f32[12,4,3,128]{3,1,2,0:T(4,128)S(1)}, /*index=5*/f32[]{:T(128)}, s32[12]{0:T(128)S(1)}, s32[12]{0:T(128)S(1)}, ...), branch_computations={%region_17.19_spmd, %region_18.22_spmd.clone} | conditional | flops 18620530 | bytes 496251 | solution.py:71
  403.3 10.4 %conditional.7 = (f32[1,4,5,128]{3,2,1,0:T(8,128)S(1)}) conditional(s32[]{:T(128)} %convert_element_type.50, () %tuple.142, (s32[4]{0:T(128)S(1)}, s32[12]{0:T(128)S(1)}, s32[]{:T(128)}, f32[2,3,8192]{2,1,0:T(4,128)S(1)}, f32[12,4,3,128]{3,1,2,0:T(4,128)S(1)}, /*index=5*/f32[]{:T(128)}, s32[12]{0:T(128)S(1)}, s32[12]{0:T(128)S(1)}, ...), branch_computations={%region_17.19_spmd, %region_18.22_spmd.clone} | conditional | flops 18620530 | bytes 496251 | solution.py:71
  415.0 10.4 %conditional.7 = (f32[1,4,5,128]{3,2,1,0:T(8,128)S(1)}) conditional(s32[]{:T(128)} %convert_element_type.50, () %tuple.142, (s32[4]{0:T(128)S(1)}, s32[12]{0:T(128)S(1)}, s32[]{:T(128)}, f32[2,3,8192]{2,1,0:T(4,128)S(1)}, f32[12,4,3,128]{3,1,2,0:T(4,128)S(1)}, /*index=5*/f32[]{:T(128)}, s32[12]{0:T(128)S(1)}, s32[12]{0:T(128)S(1)}, ...), branch_computations={%region_17.19_spmd, %region_18.22_spmd.clone} | conditional | flops 18620530 | bytes 496251 | solution.py:71
  426.7 10.4 %conditional.7 = (f32[1,4,5,128]{3,2,1,0:T(8,128)S(1)}) conditional(s32[]{:T(128)} %convert_element_type.50, () %tuple.142, (s32[4]{0:T(128)S(1)}, s32[12]{0:T(128)S(1)}, s32[]{:T(128)}, f32[2,3,8192]{2,1,0:T(4,128)S(1)}, f32[12,4,3,128]{3,1,2,0:T(4,128)S(1)}, /*index=5*/f32[]{:T(128)}, s32[12]{0:T(128)S(1)}, s32[12]{0:T(128)S(1)}, ...), branch_computations={%region_17.19_spmd, %region_18.22_spmd.clone} | conditional | flops 18620530 | bytes 496251 | solution.py:71
  438.4 10.4 %conditional.7 = (f32[1,4,5,128]{3,2,1,0:T(8,128)S(1)}) conditional(s32[]{:T(128)} %convert_element_type.50, () %tuple.142, (s32[4]{0:T(128)S(1)}, s32[12]{0:T(128)S(1)}, s32[]{:T(128)}, f32[2,3,8192]{2,1,0:T(4,128)S(1)}, f32[12,4,3,128]{3,1,2,0:T(4,128)S(1)}, /*index=5*/f32[]{:T(128)}, s32[12]{0:T(128)S(1)}, s32[12]{0:T(128)S(1)}, ...), branch_computations={%region_17.19_spmd, %region_18.22_spmd.clone} | conditional | flops 18620530 | bytes 496251 | solution.py:71
  450.1 10.4 %conditional.7 = (f32[1,4,5,128]{3,2,1,0:T(8,128)S(1)}) conditional(s32[]{:T(128)} %convert_element_type.50, () %tuple.142, (s32[4]{0:T(128)S(1)}, s32[12]{0:T(128)S(1)}, s32[]{:T(128)}, f32[2,3,8192]{2,1,0:T(4,128)S(1)}, f32[12,4,3,128]{3,1,2,0:T(4,128)S(1)}, /*index=5*/f32[]{:T(128)}, s32[12]{0:T(128)S(1)}, s32[12]{0:T(128)S(1)}, ...), branch_computations={%region_17.19_spmd, %region_18.22_spmd.clone} | conditional | flops 18620530 | bytes 496251 | solution.py:71
  461.8 10.4 %conditional.7 = (f32[1,4,5,128]{3,2,1,0:T(8,128)S(1)}) conditional(s32[]{:T(128)} %convert_element_type.50, () %tuple.142, (s32[4]{0:T(128)S(1)}, s32[12]{0:T(128)S(1)}, s32[]{:T(128)}, f32[2,3,8192]{2,1,0:T(4,128)S(1)}, f32[12,4,3,128]{3,1,2,0:T(4,128)S(1)}, /*index=5*/f32[]{:T(128)}, s32[12]{0:T(128)S(1)}, s32[12]{0:T(128)S(1)}, ...), branch_computations={%region_17.19_spmd, %region_18.22_spmd.clone} | conditional | flops 18620530 | bytes 496251 | solution.py:71
  473.6 10.4 %conditional.7 = (f32[1,4,5,128]{3,2,1,0:T(8,128)S(1)}) conditional(s32[]{:T(128)} %convert_element_type.50, () %tuple.142, (s32[4]{0:T(128)S(1)}, s32[12]{0:T(128)S(1)}, s32[]{:T(128)}, f32[2,3,8192]{2,1,0:T(4,128)S(1)}, f32[12,4,3,128]{3,1,2,0:T(4,128)S(1)}, /*index=5*/f32[]{:T(128)}, s32[12]{0:T(128)S(1)}, s32[12]{0:T(128)S(1)}, ...), branch_computations={%region_17.19_spmd, %region_18.22_spmd.clone} | conditional | flops 18620530 | bytes 496251 | solution.py:71
  485.3 10.4 %conditional.7 = (f32[1,4,5,128]{3,2,1,0:T(8,128)S(1)}) conditional(s32[]{:T(128)} %convert_element_type.50, () %tuple.142, (s32[4]{0:T(128)S(1)}, s32[12]{0:T(128)S(1)}, s32[]{:T(128)}, f32[2,3,8192]{2,1,0:T(4,128)S(1)}, f32[12,4,3,128]{3,1,2,0:T(4,128)S(1)}, /*index=5*/f32[]{:T(128)}, s32[12]{0:T(128)S(1)}, s32[12]{0:T(128)S(1)}, ...), branch_computations={%region_17.19_spmd, %region_18.22_spmd.clone} | conditional | flops 18620530 | bytes 496251 | solution.py:71
  497.0 10.4 %conditional.7 = (f32[1,4,5,128]{3,2,1,0:T(8,128)S(1)}) conditional(s32[]{:T(128)} %convert_element_type.50, () %tuple.142, (s32[4]{0:T(128)S(1)}, s32[12]{0:T(128)S(1)}, s32[]{:T(128)}, f32[2,3,8192]{2,1,0:T(4,128)S(1)}, f32[12,4,3,128]{3,1,2,0:T(4,128)S(1)}, /*index=5*/f32[]{:T(128)}, s32[12]{0:T(128)S(1)}, s32[12]{0:T(128)S(1)}, ...), branch_computations={%region_17.19_spmd, %region_18.22_spmd.clone} | conditional | flops 18620530 | bytes 496251 | solution.py:71
  508.7 10.4 %conditional.7 = (f32[1,4,5,128]{3,2,1,0:T(8,128)S(1)}) conditional(s32[]{:T(128)} %convert_element_type.50, () %tuple.142, (s32[4]{0:T(128)S(1)}, s32[12]{0:T(128)S(1)}, s32[]{:T(128)}, f32[2,3,8192]{2,1,0:T(4,128)S(1)}, f32[12,4,3,128]{3,1,2,0:T(4,128)S(1)}, /*index=5*/f32[]{:T(128)}, s32[12]{0:T(128)S(1)}, s32[12]{0:T(128)S(1)}, ...), branch_computations={%region_17.19_spmd, %region_18.22_spmd.clone} | conditional | flops 18620530 | bytes 496251 | solution.py:71
  530.3 101.3 %all-reduce.3 = (f32[]{:T(128)}, f32[]{:T(128)}) all-reduce(f32[]{:T(128)} %get-tuple-element.354, f32[]{:T(128)} %get-tuple-element.353), channel_id=1, replica_groups=mesh['line'=32,'seg'=16] {'line','seg'}, use_global_device_ids=true, to_apply=%region_25.28 | all-reduce | flops 2 | bytes 16 | tf_op jit(solution)/shard_map/psum | solution.py:159
  633.5 29.0 %all-reduce.5 = (f32[4,4]{0,1:T(4,128)S(1)}, f32[3,4]{1,0:T(4,128)S(1)}) all-reduce(f32[4,4]{0,1:T(4,128)S(1)} %convolution_bitcast_fusion.4, f32[3,4]{1,0:T(4,128)S(1)} %convolution_bitcast_fusion.3), channel_id=1, replica_groups=mesh['line'=32,'seg'=16] {'seg'}, use_global_device_ids=true, to_apply=%region_22.25 | all-reduce | flops 28 | bytes 224 | tf_op jit(solution)/shard_map/psum | solution.py:158
  (965 shorter events, 414.3 us)
Async XLA Ops:
  0.6 43.6 %copy-start = (s32[1,1,2,24]{3,2,1,0:T(2,128)S(1)}, s32[1,1,2,24]{3,2,1,0:T(2,128)}, u32[]{:S(2)}) copy-start(s32[1,1,2,24]{3,2,1,0:T(2,128)} %param.17) | copy-start | bytes 580
  36.6 29.1 %collective-permute-start.3 = (f32[3,3072]{1,0:T(4,128)S(1)}, f32[3,3072]{1,0:T(4,128)S(1)}, u32[]{:S(2)}, u32[]{:S(2)}) collective-permute-start(f32[3,3072]{1,0:T(4,128)S(1)} %get-tuple-element.436), channel_id=1, source_target_pairs={{0,16},{16,32},{32,48},{48,64},{64,80},{80,96},{96,112},{112,128},... | collective-permute-start | bytes 110600 | tf_op jit(solution)/shard_map/ppermute | solution.py:21
  38.5 27.2 %collective-permute-start.2 = (f32[3,3072]{1,0:T(4,128)S(1)}, f32[3,3072]{1,0:T(4,128)S(1)}, u32[]{:S(2)}, u32[]{:S(2)}) collective-permute-start(f32[3,3072]{1,0:T(4,128)S(1)} %get-tuple-element.435), channel_id=1, source_target_pairs={{16,0},{32,16},{48,32},{64,48},{80,64},{96,80},{112,96},{128,112},... | collective-permute-start | bytes 110600 | tf_op jit(solution)/shard_map/ppermute | solution.py:21
  44.3 21.3 %collective-permute-start = (f32[24]{0:T(128)S(1)}, f32[24]{0:T(128)S(1)}, u32[]{:S(2)}, u32[]{:S(2)}) collective-permute-start(f32[24]{0:T(128)S(1)} %get-tuple-element.439), channel_id=1, source_target_pairs={{16,0},{32,16},{48,32},{64,48},{80,64},{96,80},{112,96},{128,112},... | collective-permute-start | bytes 296 | tf_op jit(solution)/shard_map/ppermute | solution.py:21
  46.2 19.4 %collective-permute-start.1 = (f32[24]{0:T(128)S(1)}, f32[24]{0:T(128)S(1)}, u32[]{:S(2)}, u32[]{:S(2)}) collective-permute-start(f32[24]{0:T(128)S(1)} %get-tuple-element.440), channel_id=1, source_target_pairs={{0,16},{16,32},{32,48},{48,64},{64,80},{80,96},{96,112},{112,128},... | collective-permute-start | bytes 296 | tf_op jit(solution)/shard_map/ppermute | solution.py:21
  205.6 8.0 %collective-permute-start.4 = (f32[5,3072]{1,0:T(8,128)S(1)}, f32[5,3072]{1,0:T(8,128)S(1)}, u32[]{:S(2)}, u32[]{:S(2)}) collective-permute-start(f32[5,3072]{1,0:T(8,128)S(1)} %bitcast.309), channel_id=1, source_target_pairs={{0,16},{16,32},{32,48},{48,64},{64,80},{80,96},{96,112},{112,128},... | collective-permute-start | bytes 184328 | tf_op jit(solution)/shard_map/ppermute | solution.py:21
  207.5 8.0 %collective-permute-start.5 = (f32[5,3072]{1,0:T(8,128)S(1)}, f32[5,3072]{1,0:T(8,128)S(1)}, u32[]{:S(2)}, u32[]{:S(2)}) collective-permute-start(f32[5,3072]{1,0:T(8,128)S(1)} %bitcast.311), channel_id=1, source_target_pairs={{16,0},{32,16},{48,32},{64,48},{80,64},{96,80},{112,96},{128,112},... | collective-permute-start | bytes 184328 | tf_op jit(solution)/shard_map/ppermute | solution.py:21
  271.1 107.3 %collective-permute-start.7 = (f32[3,3072]{1,0:T(4,128)S(1)}, f32[3,3072]{1,0:T(4,128)S(1)}, u32[]{:S(2)}, u32[]{:S(2)}) collective-permute-start(f32[3,3072]{1,0:T(4,128)S(1)} %get-tuple-element.434), channel_id=1, source_target_pairs={{0,16},{16,32},{32,48},{48,64},{64,80},{80,96},{96,112},{112,128},... | collective-permute-start | bytes 110600 | tf_op jit(solution)/shard_map/ppermute | solution.py:21
  273.0 105.4 %collective-permute-start.6 = (f32[3,3072]{1,0:T(4,128)S(1)}, f32[3,3072]{1,0:T(4,128)S(1)}, u32[]{:S(2)}, u32[]{:S(2)}) collective-permute-start(f32[3,3072]{1,0:T(4,128)S(1)} %get-tuple-element.433), channel_id=1, source_target_pairs={{16,0},{32,16},{48,32},{64,48},{80,64},{96,80},{112,96},{128,112},... | collective-permute-start | bytes 110600 | tf_op jit(solution)/shard_map/ppermute | solution.py:21
  519.2 8.0 %collective-permute-start.8 = (f32[5,3072]{1,0:T(8,128)S(1)}, f32[5,3072]{1,0:T(8,128)S(1)}, u32[]{:S(2)}, u32[]{:S(2)}) collective-permute-start(f32[5,3072]{1,0:T(8,128)S(1)} %bitcast.310), channel_id=1, source_target_pairs={{0,16},{16,32},{32,48},{48,64},{64,80},{80,96},{96,112},{112,128},... | collective-permute-start | bytes 184328 | tf_op jit(solution)/shard_map/ppermute | solution.py:21
  521.1 8.0 %collective-permute-start.9 = (f32[5,3072]{1,0:T(8,128)S(1)}, f32[5,3072]{1,0:T(8,128)S(1)}, u32[]{:S(2)}, u32[]{:S(2)}) collective-permute-start(f32[5,3072]{1,0:T(8,128)S(1)} %bitcast.312), channel_id=1, source_target_pairs={{16,0},{32,16},{48,32},{64,48},{80,64},{96,80},{112,96},{128,112},... | collective-permute-start | bytes 184328 | tf_op jit(solution)/shard_map/ppermute | solution.py:21
where the time goes:
time: 670 us; the launch traced here: 668 us
  blocking collectives  262 us (39%)
  local copies, waits for them, and re-layouts  170 us (25%)
  matrix products  70.6 us (11%)
  other arithmetic  60.7 us (9%)
  loops' own time  59.3 us (9%)
  starting transfers between devices  35 us (5%)
    psum x2, blocking collectives, on_device(): energy_sum, share_sum = lax.psum((energy_part, share_part), ('line', 'seg'))  199 us
    gather x288, local copies, waits for them, and re-layouts  118 us
    psum x2, blocking collectives, on_device(): gram_sum, cross_sum = lax.psum((gram_matrix, cross_matrix), 'seg')  63 us
    another operation x24, loops' own time, one_turn(): return lax.cond(jnp.any(turn_cells >= 0), compute, skipped, 0)  43.1 us
    ppermute x10, starting transfers between devices, from_behind(): lax.ppermute(value, axis, [(source, source + steps) for source in range(i...  35 us
    dot_general x24, matrix products, match_block(): lax.dot_general(target, posterior, (((1,), (1,)), ((), ())), precision=la...  33.6 us
    dot_general x2, matrix products, on_device(): jnp.dot(linear_part, own_points, precision=lax.Precision.HIGHEST, preferr...  33.5 us
    gather x2, local copies, waits for them, and re-layouts, on_device(): jnp.take(own_points, safe_rows.reshape(-1), axis=1)  23 us
  transfers between devices with their start and end apart: 10, of which 4 were waited for; matrix products, arithmetic and copies ran while one was open for 3% of the time, Pallas kernels for 0%

commit v1 on v0

--- a/solution.py
+++ b/solution.py
@@ -156,7 +156,7 @@
         energy_part = jnp.sum(energy_all)
         share_part = jnp.sum(share_all)
         gram_sum, cross_sum = lax.psum((gram_matrix, cross_matrix), "seg")
-        energy_sum, share_sum = lax.psum((energy_part, share_part), ("line", "seg"))
+        energy_sum, share_sum = lax.psum(lax.psum((energy_part, share_part), "seg"), "line")
         pose_column = solve_pose(gram_sum, cross_sum, pose_column)
         spread = (energy_sum + PRIOR_TOP) / (3.0 * share_sum + PRIOR_BOTTOM)
     return (result[None, None], pose_column[:, None], spread.reshape(1))

time: 670 us -> 584 us (0.87)
  the two profiles are of different devices: /device:TPU:2 before, /device:TPU:1 now
where the time goes in v1:
time: 584 us; the launch traced here: 582 us
  blocking collectives  175 us (30%)
  local copies, waits for them, and re-layouts  171 us (29%)
  matrix products  70.6 us (12%)
  other arithmetic  60.7 us (10%)
  loops' own time  59.3 us (10%)
  starting transfers between devices  34.5 us (6%)
  waiting for transfers between devices  6.95 us (1%)
    psum x2, blocking collectives, on_device(): lax.psum(lax.psum((energy_part, share_part), 'seg'), 'line')  127 us
    gather x288, local copies, waits for them, and re-layouts  118 us
    psum x2, blocking collectives, on_device(): gram_sum, cross_sum = lax.psum((gram_matrix, cross_matrix), 'seg')  47.3 us
    another operation x24, loops' own time, one_turn(): return lax.cond(jnp.any(turn_cells >= 0), compute, skipped, 0)  43.1 us
    ppermute x10, starting transfers between devices, from_behind(): lax.ppermute(value, axis, [(source, source + steps) for source in range(i...  34.5 us
    dot_general x24, matrix products, match_block(): lax.dot_general(target, posterior, (((1,), (1,)), ((), ())), precision=la...  33.6 us
    dot_general x2, matrix products, on_device(): jnp.dot(linear_part, own_points, precision=lax.Precision.HIGHEST, preferr...  33.5 us
    gather x2, local copies, waits for them, and re-layouts, on_device(): jnp.take(own_points, safe_rows.reshape(-1), axis=1)  23 us
  transfers between devices with their start and end apart: 10, of which 2 were waited for; matrix products, arithmetic and copies ran while one was open for 3% of the time, Pallas kernels for 0%

profile of v1, /device:TPU:1, one launch (start us, length us, event | category | flops | bytes accessed | tf_op | source)
XLA Modules:
  0.0 582.1 jit_solution(9893534821868703559)
XLA Ops:
  13.1 21.8 %gather_fusion = f32[6144,3]{1,0:T(8,128)S(1)} fusion(f32[3,32768]{0,1:T(8,128)} %bitcast.285, s32[6144]{0:T(1024)S(1)} %broadcast_clamp_fusion), kind=kCustom, calls=%fused_computation | custom fusion | bytes 172032 | tf_op jit(solution)/shard_map/jit(_take)/gather | solution.py:112
  52.3 16.7 %convolution_add_fusion.1 = f32[3,32768]{1,0:T(4,128)S(1)} fusion(f32[3,3]{1,0:T(4,128)S(1)} %reshape.263, f32[3]{0:T(128)S(1)} %get-tuple-element.446, f32[1,1,3,32768]{2,3,1,0:T(8,128)} %copy.18), kind=kOutput, calls=%fused_computation.61 | convolution fusion | flops 3637248 | bytes 786480 | tf_op jit(solution)/shard_map/dot_general | solution.py:123
  69.4 139.7 %while.28 = (s32[]{:T(128)}, f32[12,4,5,128]{3,2,1,0:T(8,128)S(1)}, s32[12,4]{1,0:T(8,128)S(1)}, f32[2,3,8192]{2,1,0:T(4,128)S(1)}, f32[12,4,3,128]{3,1,2,0:T(4,128)S(1)}, /*index=5*/s32[]{:T(128)}, s32[]{:T(128)}, s32[]{:T(128)}) while((s32[]{:T(128)}, f32[12,4,5,128]{3,2,1,0:T(8,128)S(1)}, s32[12,4]{1,0:T(8,128)S(1)}, ...), condition=%wide.region_6.7_spmd.clone, body=%wide.region_0.6_spmd.clone.sunk | while | flops 18620548 | bytes 529362 | solution.py:73
  70.7 10.3 %conditional.6 = (f32[1,4,5,128]{3,2,1,0:T(8,128)S(1)}) conditional(s32[]{:T(128)} %convert_element_type.49, () %tuple.138, (s32[4]{0:T(128)S(1)}, s32[12]{0:T(128)S(1)}, s32[]{:T(128)}, f32[2,3,8192]{2,1,0:T(4,128)S(1)}, f32[12,4,3,128]{3,1,2,0:T(4,128)S(1)}, /*index=5*/s32[12]{0:T(128)S(1)}, s32[12]{0:T(128)S(1)}, s32[12]{0:T(128)S(1)}, ...), branch_computations={%region_2.2_spmd, %region_3.5_spmd.clone} | conditional | flops 18620528 | bytes 496227 | solution.py:71
  82.3 10.3 %conditional.6 = (f32[1,4,5,128]{3,2,1,0:T(8,128)S(1)}) conditional(s32[]{:T(128)} %convert_element_type.49, () %tuple.138, (s32[4]{0:T(128)S(1)}, s32[12]{0:T(128)S(1)}, s32[]{:T(128)}, f32[2,3,8192]{2,1,0:T(4,128)S(1)}, f32[12,4,3,128]{3,1,2,0:T(4,128)S(1)}, /*index=5*/s32[12]{0:T(128)S(1)}, s32[12]{0:T(128)S(1)}, s32[12]{0:T(128)S(1)}, ...), branch_computations={%region_2.2_spmd, %region_3.5_spmd.clone} | conditional | flops 18620528 | bytes 496227 | solution.py:71
  94.0 10.3 %conditional.6 = (f32[1,4,5,128]{3,2,1,0:T(8,128)S(1)}) conditional(s32[]{:T(128)} %convert_element_type.49, () %tuple.138, (s32[4]{0:T(128)S(1)}, s32[12]{0:T(128)S(1)}, s32[]{:T(128)}, f32[2,3,8192]{2,1,0:T(4,128)S(1)}, f32[12,4,3,128]{3,1,2,0:T(4,128)S(1)}, /*index=5*/s32[12]{0:T(128)S(1)}, s32[12]{0:T(128)S(1)}, s32[12]{0:T(128)S(1)}, ...), branch_computations={%region_2.2_spmd, %region_3.5_spmd.clone} | conditional | flops 18620528 | bytes 496227 | solution.py:71
  105.6 10.3 %conditional.6 = (f32[1,4,5,128]{3,2,1,0:T(8,128)S(1)}) conditional(s32[]{:T(128)} %convert_element_type.49, () %tuple.138, (s32[4]{0:T(128)S(1)}, s32[12]{0:T(128)S(1)}, s32[]{:T(128)}, f32[2,3,8192]{2,1,0:T(4,128)S(1)}, f32[12,4,3,128]{3,1,2,0:T(4,128)S(1)}, /*index=5*/s32[12]{0:T(128)S(1)}, s32[12]{0:T(128)S(1)}, s32[12]{0:T(128)S(1)}, ...), branch_computations={%region_2.2_spmd, %region_3.5_spmd.clone} | conditional | flops 18620528 | bytes 496227 | solution.py:71
  117.3 10.3 %conditional.6 = (f32[1,4,5,128]{3,2,1,0:T(8,128)S(1)}) conditional(s32[]{:T(128)} %convert_element_type.49, () %tuple.138, (s32[4]{0:T(128)S(1)}, s32[12]{0:T(128)S(1)}, s32[]{:T(128)}, f32[2,3,8192]{2,1,0:T(4,128)S(1)}, f32[12,4,3,128]{3,1,2,0:T(4,128)S(1)}, /*index=5*/s32[12]{0:T(128)S(1)}, s32[12]{0:T(128)S(1)}, s32[12]{0:T(128)S(1)}, ...), branch_computations={%region_2.2_spmd, %region_3.5_spmd.clone} | conditional | flops 18620528 | bytes 496227 | solution.py:71
  128.9 10.3 %conditional.6 = (f32[1,4,5,128]{3,2,1,0:T(8,128)S(1)}) conditional(s32[]{:T(128)} %convert_element_type.49, () %tuple.138, (s32[4]{0:T(128)S(1)}, s32[12]{0:T(128)S(1)}, s32[]{:T(128)}, f32[2,3,8192]{2,1,0:T(4,128)S(1)}, f32[12,4,3,128]{3,1,2,0:T(4,128)S(1)}, /*index=5*/s32[12]{0:T(128)S(1)}, s32[12]{0:T(128)S(1)}, s32[12]{0:T(128)S(1)}, ...), branch_computations={%region_2.2_spmd, %region_3.5_spmd.clone} | conditional | flops 18620528 | bytes 496227 | solution.py:71
  140.5 10.3 %conditional.6 = (f32[1,4,5,128]{3,2,1,0:T(8,128)S(1)}) conditional(s32[]{:T(128)} %convert_element_type.49, () %tuple.138, (s32[4]{0:T(128)S(1)}, s32[12]{0:T(128)S(1)}, s32[]{:T(128)}, f32[2,3,8192]{2,1,0:T(4,128)S(1)}, f32[12,4,3,128]{3,1,2,0:T(4,128)S(1)}, /*index=5*/s32[12]{0:T(128)S(1)}, s32[12]{0:T(128)S(1)}, s32[12]{0:T(128)S(1)}, ...), branch_computations={%region_2.2_spmd, %region_3.5_spmd.clone} | conditional | flops 18620528 | bytes 496227 | solution.py:71
  152.2 10.3 %conditional.6 = (f32[1,4,5,128]{3,2,1,0:T(8,128)S(1)}) conditional(s32[]{:T(128)} %convert_element_type.49, () %tuple.138, (s32[4]{0:T(128)S(1)}, s32[12]{0:T(128)S(1)}, s32[]{:T(128)}, f32[2,3,8192]{2,1,0:T(4,128)S(1)}, f32[12,4,3,128]{3,1,2,0:T(4,128)S(1)}, /*index=5*/s32[12]{0:T(128)S(1)}, s32[12]{0:T(128)S(1)}, s32[12]{0:T(128)S(1)}, ...), branch_computations={%region_2.2_spmd, %region_3.5_spmd.clone} | conditional | flops 18620528 | bytes 496227 | solution.py:71
  163.8 10.3 %conditional.6 = (f32[1,4,5,128]{3,2,1,0:T(8,128)S(1)}) conditional(s32[]{:T(128)} %convert_element_type.49, () %tuple.138, (s32[4]{0:T(128)S(1)}, s32[12]{0:T(128)S(1)}, s32[]{:T(128)}, f32[2,3,8192]{2,1,0:T(4,128)S(1)}, f32[12,4,3,128]{3,1,2,0:T(4,128)S(1)}, /*index=5*/s32[12]{0:T(128)S(1)}, s32[12]{0:T(128)S(1)}, s32[12]{0:T(128)S(1)}, ...), branch_computations={%region_2.2_spmd, %region_3.5_spmd.clone} | conditional | flops 18620528 | bytes 496227 | solution.py:71
  175.5 10.3 %conditional.6 = (f32[1,4,5,128]{3,2,1,0:T(8,128)S(1)}) conditional(s32[]{:T(128)} %convert_element_type.49, () %tuple.138, (s32[4]{0:T(128)S(1)}, s32[12]{0:T(128)S(1)}, s32[]{:T(128)}, f32[2,3,8192]{2,1,0:T(4,128)S(1)}, f32[12,4,3,128]{3,1,2,0:T(4,128)S(1)}, /*index=5*/s32[12]{0:T(128)S(1)}, s32[12]{0:T(128)S(1)}, s32[12]{0:T(128)S(1)}, ...), branch_computations={%region_2.2_spmd, %region_3.5_spmd.clone} | conditional | flops 18620528 | bytes 496227 | solution.py:71
  187.1 10.3 %conditional.6 = (f32[1,4,5,128]{3,2,1,0:T(8,128)S(1)}) conditional(s32[]{:T(128)} %convert_element_type.49, () %tuple.138, (s32[4]{0:T(128)S(1)}, s32[12]{0:T(128)S(1)}, s32[]{:T(128)}, f32[2,3,8192]{2,1,0:T(4,128)S(1)}, f32[12,4,3,128]{3,1,2,0:T(4,128)S(1)}, /*index=5*/s32[12]{0:T(128)S(1)}, s32[12]{0:T(128)S(1)}, s32[12]{0:T(128)S(1)}, ...), branch_computations={%region_2.2_spmd, %region_3.5_spmd.clone} | conditional | flops 18620528 | bytes 496227 | solution.py:71
  218.9 26.0 %all-reduce.6 = (f32[3,4]{1,0:T(4,128)S(1)}, f32[4,4]{0,1:T(4,128)S(1)}, f32[]{:T(128)}, f32[]{:T(128)}) all-reduce(f32[3,4]{1,0:T(4,128)S(1)} %convolution_bitcast_fusion.6, f32[4,4]{0,1:T(4,128)S(1)} %convolution_bitcast_fusion.7, f32[]{:T(128)} %get-tuple-element.356, ...), channel_id=1, replica_groups=mesh['line'=32,'seg'=16] {'seg'}, use_global_device_ids=true, to_apply=%region_10.12 | all-reduce | flops 30 | bytes 240 | tf_op jit(solution)/shard_map/psum | solution.py:158
  247.9 16.7 %convolution_add_fusion = f32[3,32768]{1,0:T(4,128)S(1)} fusion(f32[3]{0:T(128)S(1)} %slice_reduce_fusion.3, f32[3,4]{1,0:T(4,128)S(1)} %convolution_bitcast_fusion.5, f32[1,1,3,32768]{2,3,1,0:T(8,128)} %copy.18), kind=kOutput, calls=%fused_computation.60 | convolution fusion | flops 3637248 | bytes 786492 | tf_op jit(solution)/shard_map/dot_general | solution.py:123
  275.1 60.0 %all-reduce.4 = (f32[]{:T(128)}, f32[]{:T(128)}) all-reduce(f32[]{:T(128)} %get-tuple-element.405, f32[]{:T(128)} %get-tuple-element.406), channel_id=1, replica_groups=mesh['line'=32,'seg'=16] {'line'}, use_global_device_ids=true, to_apply=%region_13.16 | all-reduce | flops 2 | bytes 16 | tf_op jit(solution)/shard_map/psum | solution.py:159
  336.6 140.6 %while.29 = (s32[]{:T(128)}, f32[12,4,5,128]{3,2,1,0:T(8,128)S(1)}, s32[12,4]{1,0:T(8,128)S(1)}, f32[2,3,8192]{2,1,0:T(4,128)S(1)}, f32[12,4,3,128]{3,1,2,0:T(4,...) while((s32[]{:T(128)}, f32[12,4,5,128]{3,2,1,0:T(8,128)S(1)}, ...), condition=%wide.region_23.26_spmd.clone, body=%wide.region_17.25_spmd.clone.sunk | while | flops 18620552 | bytes 529402 | solution.py:73
  337.9 10.4 %conditional.7 = (f32[1,4,5,128]{3,2,1,0:T(8,128)S(1)}) conditional(s32[]{:T(128)} %convert_element_type.50, () %tuple.142, (s32[4]{0:T(128)S(1)}, s32[12]{0:T(128)S(1)}, s32[]{:T(128)}, f32[2,3,8192]{2,1,0:T(4,128)S(1)}, f32[12,4,3,128]{3,1,2,0:T(4,128)S(1)}, /*index=5*/f32[]{:T(128)}, s32[12]{0:T(128)S(1)}, s32[12]{0:T(128)S(1)}, ...), branch_computations={%region_19.21_spmd, %region_20.24_spmd.clone} | conditional | flops 18620530 | bytes 496251 | solution.py:71
  349.6 10.4 %conditional.7 = (f32[1,4,5,128]{3,2,1,0:T(8,128)S(1)}) conditional(s32[]{:T(128)} %convert_element_type.50, () %tuple.142, (s32[4]{0:T(128)S(1)}, s32[12]{0:T(128)S(1)}, s32[]{:T(128)}, f32[2,3,8192]{2,1,0:T(4,128)S(1)}, f32[12,4,3,128]{3,1,2,0:T(4,128)S(1)}, /*index=5*/f32[]{:T(128)}, s32[12]{0:T(128)S(1)}, s32[12]{0:T(128)S(1)}, ...), branch_computations={%region_19.21_spmd, %region_20.24_spmd.clone} | conditional | flops 18620530 | bytes 496251 | solution.py:71
  361.3 10.4 %conditional.7 = (f32[1,4,5,128]{3,2,1,0:T(8,128)S(1)}) conditional(s32[]{:T(128)} %convert_element_type.50, () %tuple.142, (s32[4]{0:T(128)S(1)}, s32[12]{0:T(128)S(1)}, s32[]{:T(128)}, f32[2,3,8192]{2,1,0:T(4,128)S(1)}, f32[12,4,3,128]{3,1,2,0:T(4,128)S(1)}, /*index=5*/f32[]{:T(128)}, s32[12]{0:T(128)S(1)}, s32[12]{0:T(128)S(1)}, ...), branch_computations={%region_19.21_spmd, %region_20.24_spmd.clone} | conditional | flops 18620530 | bytes 496251 | solution.py:71
  373.0 10.4 %conditional.7 = (f32[1,4,5,128]{3,2,1,0:T(8,128)S(1)}) conditional(s32[]{:T(128)} %convert_element_type.50, () %tuple.142, (s32[4]{0:T(128)S(1)}, s32[12]{0:T(128)S(1)}, s32[]{:T(128)}, f32[2,3,8192]{2,1,0:T(4,128)S(1)}, f32[12,4,3,128]{3,1,2,0:T(4,128)S(1)}, /*index=5*/f32[]{:T(128)}, s32[12]{0:T(128)S(1)}, s32[12]{0:T(128)S(1)}, ...), branch_computations={%region_19.21_spmd, %region_20.24_spmd.clone} | conditional | flops 18620530 | bytes 496251 | solution.py:71
  384.7 10.4 %conditional.7 = (f32[1,4,5,128]{3,2,1,0:T(8,128)S(1)}) conditional(s32[]{:T(128)} %convert_element_type.50, () %tuple.142, (s32[4]{0:T(128)S(1)}, s32[12]{0:T(128)S(1)}, s32[]{:T(128)}, f32[2,3,8192]{2,1,0:T(4,128)S(1)}, f32[12,4,3,128]{3,1,2,0:T(4,128)S(1)}, /*index=5*/f32[]{:T(128)}, s32[12]{0:T(128)S(1)}, s32[12]{0:T(128)S(1)}, ...), branch_computations={%region_19.21_spmd, %region_20.24_spmd.clone} | conditional | flops 18620530 | bytes 496251 | solution.py:71
  396.4 10.4 %conditional.7 = (f32[1,4,5,128]{3,2,1,0:T(8,128)S(1)}) conditional(s32[]{:T(128)} %convert_element_type.50, () %tuple.142, (s32[4]{0:T(128)S(1)}, s32[12]{0:T(128)S(1)}, s32[]{:T(128)}, f32[2,3,8192]{2,1,0:T(4,128)S(1)}, f32[12,4,3,128]{3,1,2,0:T(4,128)S(1)}, /*index=5*/f32[]{:T(128)}, s32[12]{0:T(128)S(1)}, s32[12]{0:T(128)S(1)}, ...), branch_computations={%region_19.21_spmd, %region_20.24_spmd.clone} | conditional | flops 18620530 | bytes 496251 | solution.py:71
  408.1 10.4 %conditional.7 = (f32[1,4,5,128]{3,2,1,0:T(8,128)S(1)}) conditional(s32[]{:T(128)} %convert_element_type.50, () %tuple.142, (s32[4]{0:T(128)S(1)}, s32[12]{0:T(128)S(1)}, s32[]{:T(128)}, f32[2,3,8192]{2,1,0:T(4,128)S(1)}, f32[12,4,3,128]{3,1,2,0:T(4,128)S(1)}, /*index=5*/f32[]{:T(128)}, s32[12]{0:T(128)S(1)}, s32[12]{0:T(128)S(1)}, ...), branch_computations={%region_19.21_spmd, %region_20.24_spmd.clone} | conditional | flops 18620530 | bytes 496251 | solution.py:71
  419.9 10.4 %conditional.7 = (f32[1,4,5,128]{3,2,1,0:T(8,128)S(1)}) conditional(s32[]{:T(128)} %convert_element_type.50, () %tuple.142, (s32[4]{0:T(128)S(1)}, s32[12]{0:T(128)S(1)}, s32[]{:T(128)}, f32[2,3,8192]{2,1,0:T(4,128)S(1)}, f32[12,4,3,128]{3,1,2,0:T(4,128)S(1)}, /*index=5*/f32[]{:T(128)}, s32[12]{0:T(128)S(1)}, s32[12]{0:T(128)S(1)}, ...), branch_computations={%region_19.21_spmd, %region_20.24_spmd.clone} | conditional | flops 18620530 | bytes 496251 | solution.py:71
  431.6 10.4 %conditional.7 = (f32[1,4,5,128]{3,2,1,0:T(8,128)S(1)}) conditional(s32[]{:T(128)} %convert_element_type.50, () %tuple.142, (s32[4]{0:T(128)S(1)}, s32[12]{0:T(128)S(1)}, s32[]{:T(128)}, f32[2,3,8192]{2,1,0:T(4,128)S(1)}, f32[12,4,3,128]{3,1,2,0:T(4,128)S(1)}, /*index=5*/f32[]{:T(128)}, s32[12]{0:T(128)S(1)}, s32[12]{0:T(128)S(1)}, ...), branch_computations={%region_19.21_spmd, %region_20.24_spmd.clone} | conditional | flops 18620530 | bytes 496251 | solution.py:71
  443.3 10.4 %conditional.7 = (f32[1,4,5,128]{3,2,1,0:T(8,128)S(1)}) conditional(s32[]{:T(128)} %convert_element_type.50, () %tuple.142, (s32[4]{0:T(128)S(1)}, s32[12]{0:T(128)S(1)}, s32[]{:T(128)}, f32[2,3,8192]{2,1,0:T(4,128)S(1)}, f32[12,4,3,128]{3,1,2,0:T(4,128)S(1)}, /*index=5*/f32[]{:T(128)}, s32[12]{0:T(128)S(1)}, s32[12]{0:T(128)S(1)}, ...), branch_computations={%region_19.21_spmd, %region_20.24_spmd.clone} | conditional | flops 18620530 | bytes 496251 | solution.py:71
  455.0 10.4 %conditional.7 = (f32[1,4,5,128]{3,2,1,0:T(8,128)S(1)}) conditional(s32[]{:T(128)} %convert_element_type.50, () %tuple.142, (s32[4]{0:T(128)S(1)}, s32[12]{0:T(128)S(1)}, s32[]{:T(128)}, f32[2,3,8192]{2,1,0:T(4,128)S(1)}, f32[12,4,3,128]{3,1,2,0:T(4,128)S(1)}, /*index=5*/f32[]{:T(128)}, s32[12]{0:T(128)S(1)}, s32[12]{0:T(128)S(1)}, ...), branch_computations={%region_19.21_spmd, %region_20.24_spmd.clone} | conditional | flops 18620530 | bytes 496251 | solution.py:71
  466.7 10.4 %conditional.7 = (f32[1,4,5,128]{3,2,1,0:T(8,128)S(1)}) conditional(s32[]{:T(128)} %convert_element_type.50, () %tuple.142, (s32[4]{0:T(128)S(1)}, s32[12]{0:T(128)S(1)}, s32[]{:T(128)}, f32[2,3,8192]{2,1,0:T(4,128)S(1)}, f32[12,4,3,128]{3,1,2,0:T(4,128)S(1)}, /*index=5*/f32[]{:T(128)}, s32[12]{0:T(128)S(1)}, s32[12]{0:T(128)S(1)}, ...), branch_computations={%region_19.21_spmd, %region_20.24_spmd.clone} | conditional | flops 18620530 | bytes 496251 | solution.py:71
  486.9 21.3 %all-reduce.5 = (f32[4,4]{0,1:T(4,128)S(1)}, f32[3,4]{1,0:T(4,128)S(1)}, f32[]{:T(128)}, f32[]{:T(128)}) all-reduce(f32[4,4]{0,1:T(4,128)S(1)} %convolution_bitcast_fusion.4, f32[3,4]{1,0:T(4,128)S(1)} %convolution_bitcast_fusion.3, f32[]{:T(128)} %get-tuple-element.354, ...), channel_id=1, replica_groups=mesh['line'=32,'seg'=16] {'seg'}, use_global_device_ids=true, to_apply=%region_24.27 | all-reduce | flops 30 | bytes 240 | tf_op jit(solution)/shard_map/psum | solution.py:158
  508.1 67.3 %all-reduce.3 = (f32[]{:T(128)}, f32[]{:T(128)}) all-reduce(f32[]{:T(128)} %get-tuple-element.401, f32[]{:T(128)} %get-tuple-element.402), channel_id=1, replica_groups=mesh['line'=32,'seg'=16] {'line'}, use_global_device_ids=true, to_apply=%region_28.31 | all-reduce | flops 2 | bytes 16 | tf_op jit(solution)/shard_map/psum | solution.py:159
  (965 shorter events, 416.3 us)
Async XLA Ops:
  0.6 46.0 %copy-start = (s32[1,1,2,24]{3,2,1,0:T(2,128)S(1)}, s32[1,1,2,24]{3,2,1,0:T(2,128)}, u32[]{:S(2)}) copy-start(s32[1,1,2,24]{3,2,1,0:T(2,128)} %param.17) | copy-start | bytes 580
  36.6 32.7 %collective-permute-start.3 = (f32[3,3072]{1,0:T(4,128)S(1)}, f32[3,3072]{1,0:T(4,128)S(1)}, u32[]{:S(2)}, u32[]{:S(2)}) collective-permute-start(f32[3,3072]{1,0:T(4,128)S(1)} %get-tuple-element.440), channel_id=1, source_target_pairs={{0,16},{16,32},{32,48},{48,64},{64,80},{80,96},{96,112},{112,128},... | collective-permute-start | bytes 110600 | tf_op jit(solution)/shard_map/ppermute | solution.py:21
  41.1 28.1 %collective-permute-start.2 = (f32[3,3072]{1,0:T(4,128)S(1)}, f32[3,3072]{1,0:T(4,128)S(1)}, u32[]{:S(2)}, u32[]{:S(2)}) collective-permute-start(f32[3,3072]{1,0:T(4,128)S(1)} %get-tuple-element.439), channel_id=1, source_target_pairs={{16,0},{32,16},{48,32},{64,48},{80,64},{96,80},{112,96},{128,112},... | collective-permute-start | bytes 110600 | tf_op jit(solution)/shard_map/ppermute | solution.py:21
  46.6 22.5 %collective-permute-start = (f32[24]{0:T(128)S(1)}, f32[24]{0:T(128)S(1)}, u32[]{:S(2)}, u32[]{:S(2)}) collective-permute-start(f32[24]{0:T(128)S(1)} %get-tuple-element.443), channel_id=1, source_target_pairs={{16,0},{32,16},{48,32},{64,48},{80,64},{96,80},{112,96},{128,112},... | collective-permute-start | bytes 296 | tf_op jit(solution)/shard_map/ppermute | solution.py:21
  48.6 20.6 %collective-permute-start.1 = (f32[24]{0:T(128)S(1)}, f32[24]{0:T(128)S(1)}, u32[]{:S(2)}, u32[]{:S(2)}) collective-permute-start(f32[24]{0:T(128)S(1)} %get-tuple-element.444), channel_id=1, source_target_pairs={{0,16},{16,32},{32,48},{48,64},{64,80},{80,96},{96,112},{112,128},... | collective-permute-start | bytes 296 | tf_op jit(solution)/shard_map/ppermute | solution.py:21
  209.2 4.5 collective-permute-start.4
  211.1 5.9 %collective-permute-start.5 = (f32[5,3072]{1,0:T(8,128)S(1)}, f32[5,3072]{1,0:T(8,128)S(1)}, u32[]{:S(2)}, u32[]{:S(2)}) collective-permute-start(f32[5,3072]{1,0:T(8,128)S(1)} %bitcast.310), channel_id=1, source_target_pairs={{16,0},{32,16},{48,32},{64,48},{80,64},{96,80},{112,96},{128,112},... | collective-permute-start | bytes 184328 | tf_op jit(solution)/shard_map/ppermute | solution.py:21
  264.7 71.8 %collective-permute-start.7 = (f32[3,3072]{1,0:T(4,128)S(1)}, f32[3,3072]{1,0:T(4,128)S(1)}, u32[]{:S(2)}, u32[]{:S(2)}) collective-permute-start(f32[3,3072]{1,0:T(4,128)S(1)} %get-tuple-element.438), channel_id=1, source_target_pairs={{0,16},{16,32},{32,48},{48,64},{64,80},{80,96},{96,112},{112,128},... | collective-permute-start | bytes 110600 | tf_op jit(solution)/shard_map/ppermute | solution.py:21
  273.0 63.4 %collective-permute-start.6 = (f32[3,3072]{1,0:T(4,128)S(1)}, f32[3,3072]{1,0:T(4,128)S(1)}, u32[]{:S(2)}, u32[]{:S(2)}) collective-permute-start(f32[3,3072]{1,0:T(4,128)S(1)} %get-tuple-element.437), channel_id=1, source_target_pairs={{16,0},{32,16},{48,32},{64,48},{80,64},{96,80},{112,96},{128,112},... | collective-permute-start | bytes 110600 | tf_op jit(solution)/shard_map/ppermute | solution.py:21
  477.2 4.4 collective-permute-start.8
  479.2 5.9 %collective-permute-start.9 = (f32[5,3072]{1,0:T(8,128)S(1)}, f32[5,3072]{1,0:T(8,128)S(1)}, u32[]{:S(2)}, u32[]{:S(2)}) collective-permute-start(f32[5,3072]{1,0:T(8,128)S(1)} %bitcast.312), channel_id=1, source_target_pairs={{16,0},{32,16},{48,32},{64,48},{80,64},{96,80},{112,96},{128,112},... | collective-permute-start | bytes 184328 | tf_op jit(solution)/shard_map/ppermute | solution.py:21
